TPU v7x, 128 devices: a whole 4x4x4 slice. The times are simulated.
128 devices in a mesh: row: 16 (over z_hi, x, core), col: 8 (over y, z_lo).
Axes of the slice: x: 4, y: 4, z: 4 (z_hi: 2, z_lo: 2; z = z_hi * 2 + z_lo), core: 2. Of those that a mesh axis runs over, the one named last changes fastest.
Arguments:
- before_scan: float32 [4, 4096, 8192], P(None, 'row', 'col'), may hold values from -40 to 40
- after_scan: float32 [4, 4096, 8192], P(None, 'row', 'col'), may hold values from -40 to 40
- drift_offsets: int32 [2, 4, 16, 8], P(None, None, 'row', 'col'), may hold values from -128 to 128, as said below
- drift_fractions: int32 [2, 4, 16, 8], P(None, None, 'row', 'col'), may hold values from 0 to 255
Outputs:
- band_field: float32 [4, 4096, 8192], P(None, 'row', 'col')
- slope_field: float32 [4, 4096, 8192], P(None, 'row', 'col')
- surface_params: float32 [2, 4], replicated
Inputs may be any that keep to these rules, and one draw needn't show every extreme that they name: `drift_offsets`: for every scan and tile, the cells a tile reads (its own cells shifted by its offsets, widened by one row and column before and two after) lie inside the window. In every scan the first tile has offsets 128, 128 and the last tile minus 128, minus 128.
All inputs are finite; a program needn't handle non-finite values.
Results may differ from a plain program's by a relative error of at most 0.00014.
Values sent between devices are 32-bit elements; how exact they have to be, the bound alone decides.
No kernel may reach another device: no remote copies, remote signals or barrier semaphores. Data moves between devices by JAX's collectives and lax.ppermute only.
A program may use at most 128 MiB of HBM per device.

v0:
```python
import math
import jax
import jax.numpy as jnp
from jax import lax
from jax.sharding import PartitionSpec as P

LS = 5
SR = 4
LCUT = 1600
BLOCK = 16
DRIFT = 128
ALPHA = math.sqrt(math.log(2.0) / math.pi)
SPACING = 0.5
EPSILON = 1e-06
HIGHEST = lax.Precision.HIGHEST


def with_halo(value, sides, width):
    for axis, dim in sides:
        count, length = (lax.axis_size(axis), value.shape[dim])
        up = [(i, (i + 1) % count) for i in range(count - 1)]
        down = [(j, i) for i, j in up]
        last = lax.slice_in_dim(value, length - width, length, axis=dim)
        leading = lax.slice_in_dim(value, 0, width, axis=dim)
        before = lax.ppermute(last, axis, up)
        after = lax.ppermute(leading, axis, down)
        value = jnp.concatenate([before, value, after], axis=dim)
    return value


def cubic_weights(fraction):
    position = fraction.astype(jnp.float32) / 256.0
    square = position * position
    cube_term = square * position
    return (
        0.5 * (2.0 * square - cube_term - position),
        0.5 * (3.0 * cube_term - 5.0 * square + 2.0),
        0.5 * (4.0 * square - 3.0 * cube_term + position),
        0.5 * (cube_term - square),
    )


def interpolate(window, row_taps, col_taps):
    height = window.shape[0] - 3
    length = window.shape[1] - 3
    across = (
        row_taps[0] * window[0:height]
        + row_taps[1] * window[1 : height + 1]
        + row_taps[2] * window[2 : height + 2]
        + row_taps[3] * window[3 : height + 3]
    )
    return (
        col_taps[0] * across[:, 0:length]
        + col_taps[1] * across[:, 1 : length + 1]
        + col_taps[2] * across[:, 2 : length + 2]
        + col_taps[3] * across[:, 3 : length + 3]
    )


def resample(after_scan, drift_offsets, drift_fractions):
    height, length = (after_scan.shape[1], after_scan.shape[2])
    margin = DRIFT + 2
    widened = with_halo(after_scan, (("row", 1), ("col", 2)), margin)
    row_taps = jnp.stack(cubic_weights(drift_fractions[0, :, 0, 0]), axis=-1)
    col_taps = jnp.stack(cubic_weights(drift_fractions[1, :, 0, 0]), axis=-1)

    def one_scan(window, row_shift, col_shift, row_weights, col_weights):
        source = lax.dynamic_slice(
            window, (margin - 1 + row_shift, margin - 1 + col_shift), (height + 3, length + 3)
        )
        return interpolate(source, row_weights, col_weights)

    return jax.vmap(one_scan)(
        widened, drift_offsets[0, :, 0, 0], drift_offsets[1, :, 0, 0], row_taps, col_taps
    )


def short_taps():
    return [math.exp(-math.pi * (offset / (ALPHA * LS)) ** 2) for offset in range(-SR, SR + 1)]


def short_filter(widened, height, length):
    kernel_taps = short_taps()
    column_index = (
        lax.axis_index("col") * length - SR + jnp.arange(length + 2 * SR, dtype=jnp.int32)
    )
    column_inside = ((column_index >= 0) & (column_index < length * lax.axis_size("col"))).astype(
        jnp.float32
    )
    summed = kernel_taps[0] * widened[:, :, 0:length]
    weight = kernel_taps[0] * column_inside[0:length]
    for offset in range(1, 2 * SR + 1):
        summed = summed + kernel_taps[offset] * widened[:, :, offset : offset + length]
        weight = weight + kernel_taps[offset] * column_inside[offset : offset + length]
    across = summed / weight
    row_index = lax.axis_index("row") * height - SR + jnp.arange(height + 2 * SR, dtype=jnp.int32)
    row_inside = ((row_index >= 0) & (row_index < height * lax.axis_size("row"))).astype(
        jnp.float32
    )
    summed = kernel_taps[0] * across[:, 0:height, :]
    weight = kernel_taps[0] * row_inside[0:height]
    for offset in range(1, 2 * SR + 1):
        summed = summed + kernel_taps[offset] * across[:, offset : offset + height, :]
        weight = weight + kernel_taps[offset] * row_inside[offset : offset + height]
    return summed / weight[:, None]


def coarse_means(surface):
    scans, height, length = surface.shape
    return surface.reshape(scans, height // BLOCK, BLOCK, length // BLOCK, BLOCK).mean(axis=(2, 4))


def gauss_block(source, target):
    distance = ((source[:, None] - target[None, :]) * BLOCK).astype(jnp.float32) / (ALPHA * LCUT)
    return jnp.exp(-math.pi * distance * distance)


def long_cols(coarse):
    width = coarse.shape[2]
    target = lax.axis_index("col") * width + jnp.arange(width, dtype=jnp.int32)
    portion = lax.all_gather(coarse, "col", axis=2, tiled=True)
    source = jnp.arange(portion.shape[2], dtype=jnp.int32)
    matrix = gauss_block(source, target)
    summed = jnp.einsum("frk,kc->frc", portion, matrix, precision=HIGHEST)
    weight = jnp.sum(matrix, axis=0)
    return summed / weight


def long_rows(surface):
    rows_here = surface.shape[1]
    target = lax.axis_index("row") * rows_here + jnp.arange(rows_here, dtype=jnp.int32)
    portion = lax.all_gather(surface, "row", axis=1, tiled=True)
    source = jnp.arange(portion.shape[1], dtype=jnp.int32)
    matrix = gauss_block(target, source)
    summed = jnp.einsum("rk,fkc->frc", matrix, portion, precision=HIGHEST)
    weight = jnp.sum(matrix, axis=1)
    return summed / weight[:, None]


def upsample_matrix(fine_index, coarse_index, coarse_count):
    numerator = 2 * fine_index + 1 - BLOCK
    lower_index = numerator // (2 * BLOCK)
    fraction = (numerator - lower_index * (2 * BLOCK)).astype(jnp.float32) / (2.0 * BLOCK)
    outside = (lower_index < 0) | (lower_index >= coarse_count - 1)
    fraction = jnp.where(outside, jnp.zeros_like(fraction), fraction)
    lower_index = jnp.clip(lower_index, 0, coarse_count - 1)
    first_part = (coarse_index[None, :] == lower_index[:, None]).astype(jnp.float32) * (
        1.0 - fraction
    )[:, None]
    second_part = (coarse_index[None, :] == (lower_index + 1)[:, None]).astype(
        jnp.float32
    ) * fraction[:, None]
    return first_part + second_part


def upsample(wavy_coarse, height, length):
    coarse_rows, coarse_cols = (wavy_coarse.shape[1], wavy_coarse.shape[2])
    widened_coarse = with_halo(wavy_coarse, (("row", 1), ("col", 2)), 1)
    row_fine = lax.axis_index("row") * height + jnp.arange(height, dtype=jnp.int32)
    row_blocks = (
        lax.axis_index("row") * coarse_rows - 1 + jnp.arange(coarse_rows + 2, dtype=jnp.int32)
    )
    col_fine = lax.axis_index("col") * length + jnp.arange(length, dtype=jnp.int32)
    col_blocks = (
        lax.axis_index("col") * coarse_cols - 1 + jnp.arange(coarse_cols + 2, dtype=jnp.int32)
    )
    row_up = upsample_matrix(row_fine, row_blocks, coarse_rows * lax.axis_size("row"))
    col_up = upsample_matrix(col_fine, col_blocks, coarse_cols * lax.axis_size("col"))
    row_mixed = jnp.einsum("pa,sab->spb", row_up, widened_coarse, precision=HIGHEST)
    return jnp.einsum("spb,qb->spq", row_mixed, col_up, precision=HIGHEST)


def slopes(surface):
    height, length = (surface.shape[1], surface.shape[2])
    bordered = with_halo(surface, (("row", 1), ("col", 2)), 1)
    column_index = lax.axis_index("col") * length + jnp.arange(length, dtype=jnp.int32)
    row_index = lax.axis_index("row") * height + jnp.arange(height, dtype=jnp.int32)
    column_mask = (
        (column_index >= 1) & (column_index <= length * lax.axis_size("col") - 2)
    ).astype(jnp.float32)
    row_mask = ((row_index >= 1) & (row_index <= height * lax.axis_size("row") - 2)).astype(
        jnp.float32
    )
    along_cols = (bordered[:, 1:-1, 2:] - bordered[:, 1:-1, :-2]) / (2.0 * SPACING) * column_mask
    along_rows = (
        (bordered[:, 2:, 1:-1] - bordered[:, :-2, 1:-1]) / (2.0 * SPACING) * row_mask[:, None]
    )
    return along_cols * along_cols + along_rows * along_rows


def body(before_scan, after_scan, drift_offsets, drift_fractions):
    height, length = (before_scan.shape[1], before_scan.shape[2])
    shifted = resample(after_scan, drift_offsets, drift_fractions)
    difference = before_scan - shifted
    widened = with_halo(difference, (("row", 1), ("col", 2)), SR)
    smooth = short_filter(widened, height, length)
    coarse = coarse_means(smooth)
    wavy_coarse = long_rows(long_cols(coarse))
    waviness = upsample(wavy_coarse, height, length)
    band_field = smooth - waviness
    slope_field = slopes(band_field)
    height_sq = jnp.sum(band_field * band_field, axis=(1, 2))
    slope_sum = jnp.sum(slope_field, axis=(1, 2))
    height_all, slope_all = lax.psum((height_sq, slope_sum), ("row", "col"))
    total_cells = height * lax.axis_size("row") * length * lax.axis_size("col")
    surface_params = jnp.sqrt(jnp.stack([height_all, slope_all]) / total_cells + EPSILON)
    return (band_field, slope_field, surface_params)


def solution(mesh):
    in_specs = (
        P(None, "row", "col"),
        P(None, "row", "col"),
        P(None, None, "row", "col"),
        P(None, None, "row", "col"),
    )
    out_specs = (P(None, "row", "col"), P(None, "row", "col"), P())
    return jax.shard_map(body, mesh=mesh, in_specs=in_specs, out_specs=out_specs, check_vma=False)
```

profile of v0, /device:TPU:1, one launch (start us, length us, event | category | flops | bytes accessed | tf_op | source)
XLA Modules:
  0.0 455.7 jit_solution(10664465496469987918)
XLA Ops:
  0.6 3.2 fusion.118
  3.9 1.4 copy.42
  5.3 4.5 collective-permute-start
  9.8 2.7 copy.43
  12.5 2.0 collective-permute-start.1
  14.5 5.2 %copy.28 = f32[4,256,1024]{1,0,2:T(4,128)} copy(f32[4,256,1024]{2,1,0:T(8,128)} %param.5) | data formatting | bytes 8388608 | tf_op args[1]
  19.9 13.1 %collective-permute-done = f32[4,130,1024]{2,0,1:T(4,128)} collective-permute-done((f32[4,130,1024]{2,0,1:T(4,128)S(1)}, f32[4,130,1024]{2,0,1:T(4,128)}, u32[]{:S(2)}, u32[]{:S(2)}) %collective-permute-start) | collective-permute-done | bytes 2129952 | tf_op jit(solution)/shard_map/ppermute | solution.py:25
  33.1 6.2 %copy.27 = f32[4,130,1024]{1,0,2:T(4,128)} copy(f32[4,130,1024]{2,0,1:T(4,128)} %collective-permute-done) | data formatting | bytes 4259840 | tf_op jit(solution)/shard_map/ppermute | solution.py:25
  39.3 1.3 collective-permute-done.1
  40.6 6.2 %copy.29 = f32[4,130,1024]{1,0,2:T(4,128)} copy(f32[4,130,1024]{2,0,1:T(4,128)} %collective-permute-done.1) | data formatting | bytes 4259840 | tf_op jit(solution)/shard_map/ppermute | solution.py:26
  46.8 3.5 pad_maximum_fusion.13
  50.3 3.8 collective-permute-start.2
  54.1 1.5 collective-permute-start.3
  56.2 40.7 %collective-permute-done.2 = f32[4,516,130]{1,0,2:T(4,128)S(1)} collective-permute-done((f32[4,516,130]{1,0,2:T(4,128)S(1)}, f32[4,516,130]{1,0,2:T(4,128)S(1)}, u32[]{:S(2)}, u32[]{:S(2)}) %collective-permute-start.2) | collective-permute-done | bytes 1073312 | tf_op jit(solution)/shard_map/ppermute | solution.py:25
  97.0 29.5 %pad_maximum_fusion = f32[4,516,1284]{1,0,2:T(4,128)} fusion(f32[4,516,130]{1,0,2:T(4,128)S(1)} %collective-permute-done.3, f32[4,130,1024]{1,0,2:T(4,128)} %copy.29, f32[4,256,1024]{1,0,2:T(4,128)S(1)} %copy-done.2, f32[4,130,1024]{1,0,2:T(4,128)} %copy.27, f32[4,516,130]{1,0,2:T(4,128)S(1)} %collective-permute-done.2), kind=kLoop, calls=%fused_computation.2 | loop fusion | flops 10600704 | bytes 21201408 | tf_op jit(solution)/shard_map/concatenate | solution.py:27
  126.4 15.3 %copy.30 = f32[4,516,1284]{2,1,0:T(8,128)} copy(f32[4,516,1284]{1,0,2:T(4,128)} %pad_maximum_fusion) | data formatting | bytes 21201408
  141.7 21.6 %while.1 = (s32[]{:T(128)}, f32[4,516,1284]{2,1,0:T(8,128)}, s32[4,3]{1,0:T(4,128)S(1)}, f32[4,259,1027]{2,1,0:T(8,128)}, s32[]{:T(128)}) while((s32[]{:T(128)}, f32[4,516,1284]{2,1,0:T(8,128)}, s32[4,3]{1,0:T(4,128)S(1)}, f32[4,259,1027]{2,1,0:T(8,128)}, s32[]{:T(128)}) %tuple.51), condition=%wide.while_cond, body=%wide.while_body.sunk | while | flops 2 | bytes 2435185 | solution.py:68
  141.7 0.7 fusion.124
  142.3 4.8 %dynamic-slice_dynamic-update-slice_fusion.2 = f32[4,259,1027]{2,1,0:T(8,128)} fusion(f32[4,259,1027]{2,1,0:T(8,128)} %get-tuple-element.118, s32[]{:T(128)} %get-tuple-element.115, f32[4,516,1284]{2,1,0:T(8,128)} %get-tuple-element.121, s32[]{:T(128)} %bitcast.84, s32[]{:T(128)} %bitcast.85, s32[]{:T(128)} %bitcast.86), kind=kLoop, calls=%fused_computation.clone.1 | loop fusion | bytes 2435072 | tf_op jit(solution)/shard_map/vmap()/gather
  147.1 0.7 fusion.124
  147.8 4.7 %dynamic-slice_dynamic-update-slice_fusion.2 = f32[4,259,1027]{2,1,0:T(8,128)} fusion(f32[4,259,1027]{2,1,0:T(8,128)} %get-tuple-element.118, s32[]{:T(128)} %get-tuple-element.115, f32[4,516,1284]{2,1,0:T(8,128)} %get-tuple-element.121, s32[]{:T(128)} %bitcast.84, s32[]{:T(128)} %bitcast.85, s32[]{:T(128)} %bitcast.86), kind=kLoop, calls=%fused_computation.clone.1 | loop fusion | bytes 2435072 | tf_op jit(solution)/shard_map/vmap()/gather
  152.5 0.7 fusion.124
  153.1 4.7 %dynamic-slice_dynamic-update-slice_fusion.2 = f32[4,259,1027]{2,1,0:T(8,128)} fusion(f32[4,259,1027]{2,1,0:T(8,128)} %get-tuple-element.118, s32[]{:T(128)} %get-tuple-element.115, f32[4,516,1284]{2,1,0:T(8,128)} %get-tuple-element.121, s32[]{:T(128)} %bitcast.84, s32[]{:T(128)} %bitcast.85, s32[]{:T(128)} %bitcast.86), kind=kLoop, calls=%fused_computation.clone.1 | loop fusion | bytes 2435072 | tf_op jit(solution)/shard_map/vmap()/gather
  157.8 0.7 fusion.124
  158.5 4.7 %dynamic-slice_dynamic-update-slice_fusion.2 = f32[4,259,1027]{2,1,0:T(8,128)} fusion(f32[4,259,1027]{2,1,0:T(8,128)} %get-tuple-element.118, s32[]{:T(128)} %get-tuple-element.115, f32[4,516,1284]{2,1,0:T(8,128)} %get-tuple-element.121, s32[]{:T(128)} %bitcast.84, s32[]{:T(128)} %bitcast.85, s32[]{:T(128)} %bitcast.86), kind=kLoop, calls=%fused_computation.clone.1 | loop fusion | bytes 2435072 | tf_op jit(solution)/shard_map/vmap()/gather
  163.2 9.2 %multiply_add_fusion = f32[4,256,1027]{2,1,0:T(8,128)S(1)} fusion(f32[4,259,1027]{2,1,0:T(8,128)} %get-tuple-element.10, f32[4]{0:T(128)S(1)} %get-tuple-element.67, f32[4]{0:T(128)S(1)} %get-tuple-element.62, f32[4]{0:T(128)S(1)} %get-tuple-element.64, f32[4]{0:T(128)S(1)} %get-tuple-element.63), kind=kLoop, calls=%fused_computation.5 | loop fusion | flops 7361536 | bytes 21033024 | tf_op jit(solution)/shard_map/vmap()/add | solution.py:47
  172.5 3.4 fusion.25
  176.0 17.8 %collective-permute-start.4 = (f32[4,4,1024]{2,1,0:T(4,128)S(1)}, f32[4,4,1024]{2,1,0:T(4,128)S(1)}, u32[]{:S(2)}, u32[]{:S(2)}) collective-permute-start(f32[4,4,1024]{2,1,0:T(4,128)S(1)} %get-tuple-element.53), channel_id=1, source_target_pairs={{0,8},{8,16},{16,24},{24,32},{32,40},{40,48},{48,56},{56,64},{64,7... | collective-permute-start | bytes 196616 | tf_op jit(solution)/shard_map/ppermute | solution.py:25
  193.8 1.9 collective-permute-start.5
  195.8 3.6 collective-permute-done.5
  199.4 0.6 pad_maximum_fusion.2
  200.2 0.3 copy.32
  200.4 4.1 collective-permute-start.6
  204.6 0.3 copy.34
  204.8 1.5 collective-permute-start.7
  206.6 3.0 collective-permute-done.7
  209.9 7.4 %maximum_maximum_fusion = (f32[4,264,1028]{2,1,0:T(8,128)S(1)}, f32[4,264,1028]{2,1,0:T(8,128)}) fusion(f32[4,4,1024]{2,1,0:T(4,128)S(1)} %collective-permute-done.5, f32[4,256,1024]{2,1,0:T(8,128)} %copy-done, f32[4,4,1024]{2,1,0:T(4,128)S(1)} %collective-permute-done.4, f32[4,264,4]{2,1,0:T(8,128)S(1)} %copy.33, f32[4,264,4]{2,1,0:T(8,128)S(1)} %copy.35), kind=kLoop, calls=%fused_computation.3 | loop fusion | flops 6513408 | bytes 13043712 | tf_op jit(solution)/shard_map/concatenate | solution.py:27
  217.3 15.3 %fusion.1 = f32[4,264,1024]{2,1,0:T(8,128)S(1)} fusion(f32[4,264,1028]{2,1,0:T(8,128)} %get-tuple-element.45, f32[4,264,1028]{2,1,0:T(8,128)S(1)} %get-tuple-element.44, f32[1024]{0:T(1024)S(1)} %fusion.80, f32[4,4,1024]{2,1,0:T(4,128)S(1)} %collective-permute-done.5, f32[4,256,1024]{2,1,0:T(8,128)} %copy-done, f32[4,4,1024]{2,1,0:T(4,128)S(1)} %collective-permute-done.4), kind=kLoop, calls=%fused_computation.8 | loop fusion | flops 20545536 | bytes 43257856 | tf_op jit(solution)/shard_map/div | solution.py:95
  232.7 5.7 %fusion.17 = f32[4,256,1024]{2,1,0:T(8,128)} fusion(f32[4,264,1024]{2,1,0:T(8,128)S(1)} %fusion.1, f32[256]{0:T(256)S(1)} %multiply_add_fusion.3), kind=kLoop, calls=%fused_computation.41 | loop fusion | flops 17825792 | bytes 41944064 | tf_op jit(solution)/shard_map/div | solution.py:105
  238.3 19.0 %reshape.249 = f32[4,16,16,64,16]{4,3,2,1,0:T(8,128)} reshape(f32[4,256,1024]{2,1,0:T(8,128)} %fusion.17) | data formatting | bytes 8388608 | tf_op jit(solution)/shard_map/reshape | solution.py:110
  257.3 12.2 %reduce_sum.45 = f32[4,16,64]{2,1,0:T(8,128)S(1)} reduce(f32[4,16,16,64,16]{4,3,2,1,0:T(8,128)} %reshape.249, f32[]{:T(128)} %constant.64.clone.1), dimensions={2,4}, to_apply=%region_0.0 | reduce | flops 1044480 | bytes 4210692 | tf_op jit(solution)/shard_map/reduce_sum | solution.py:110
  269.6 27.9 %all_gather.6 = f32[4,16,512]{1,0,2:T(4,128)S(1)} all-gather(f32[4,16,64]{1,0,2:T(4,128)S(1)} %copy.36), channel_id=1, replica_groups=mesh['row'=16,'col'=8] {'col'}, dimensions={2}, use_global_device_ids=true | all-gather | bytes 147456 | tf_op jit(solution)/shard_map/all_gather | solution.py:121
  297.5 1.8 convolution_divide_fusion
  299.3 27.6 %all_gather.7 = f32[4,256,64]{2,1,0:T(8,128)S(1)} all-gather(f32[4,16,64]{2,1,0:T(8,128)S(1)} %convolution_divide_fusion), channel_id=1, replica_groups=mesh['row'=16,'col'=8] {'row'}, dimensions={1}, use_global_device_ids=true | all-gather | bytes 278528 | tf_op jit(solution)/shard_map/all_gather | solution.py:132
  326.9 0.4 fusion.28
  327.3 1.9 collective-permute-start.8
  329.3 2.4 collective-permute-start.9
  331.7 2.5 collective-permute-done.9
  334.3 1.8 collective-permute-start.10
  336.1 1.6 collective-permute-start.11
  337.7 3.2 collective-permute-done.11
  340.9 0.6 convolution_bitcast_fusion
  341.5 6.0 %convolution_subtract_fusion = f32[4,256,1024]{2,1,0:T(8,128)S(1)} fusion(f32[4,256,1024]{2,1,0:T(8,128)} %fusion.17, f32[4,256,66]{1,2,0:T(8,128)S(1)} %convolution_bitcast_fusion, f32[1024]{0:T(1024)S(1)} %get-tuple-element.71, s32[1024]{0:T(1024)S(1)} %get-tuple-element.74, f32[1024]{0:T(1024)S(1)} %get-tuple-element.72, ...), kind=kOutput, calls=%fused_computation.65 | convolution fusion | flops 831858688 | bytes 8675592 | tf_op jit(solution)/shard_map/spb,qb->spq/dot_general | solution.py:170
  347.5 3.4 collective-permute-start.12
  350.9 1.9 collective-permute-start.13
  352.9 3.1 collective-permute-done.13
  356.2 0.3 copy.38
  356.5 1.3 collective-permute-start.14
  357.8 0.3 copy.40
  358.1 4.0 collective-permute-start.15
  362.3 0.5 collective-permute-done.15
  363.0 13.9 %fusion.112 = (f32[4]{0:T(128)S(1)}, f32[4,256,1024]{2,1,0:T(8,128)}, f32[4]{0:T(128)S(1)}) fusion(f32[256]{0:T(256)S(1)} %and_convert_fusion, f32[4,256,1024]{2,1,0:T(8,128)} %copy-done.1, f32[4,1,1024]{2,1,0:T(1,128)S(1)} %collective-permute-done.12, f32[4,1,1024]{2,1,0:T(1,128)S(1)} %collective-permute-done.13, f32[1024]{0:T(1024)S(1)} %fusion.92, ...), kind=kLoop, calls=%fused_computation.219 | loop fusion | flops 18874360 | bytes 8434784 | tf_op jit(solution)/shard_map/reduce_sum | solution.py:203
  377.0 78.1 %all-reduce = (f32[1,4]{1,0:T(1,128)S(1)}, f32[1,4]{1,0:T(1,128)S(1)}) all-reduce(f32[1,4]{1,0:T(1,128)S(1)} %bitcast.87, f32[1,4]{1,0:T(1,128)S(1)} %bitcast.88), channel_id=1, replica_groups=mesh['row'=16,'col'=8] {'row','col'}, use_global_device_ids=true, to_apply=%region_6.7 | all-reduce | flops 8 | bytes 64 | tf_op jit(solution)/shard_map/psum | solution.py:204
  455.1 0.6 fusion.98
  (58 shorter events, 2.5 us)
Async XLA Ops:
  5.3 27.8 %collective-permute-start = (f32[4,130,1024]{2,0,1:T(4,128)S(1)}, f32[4,130,1024]{2,0,1:T(4,128)}, u32[]{:S(2)}, u32[]{:S(2)}) collective-permute-start(f32[4,130,1024]{2,0,1:T(4,128)S(1)} %copy.42), channel_id=1, source_target_pairs={{0,8},{8,16},{16,24},{24,32},{32,40},{40,48},{48,56},{56,64},{64,7... | collective-permute-start | bytes 6389768 | tf_op jit(solution)/shard_map/ppermute | solution.py:25
  12.5 7.3 %copy-start.5 = (s32[2,4,1,1]{1,3,2,0:T(1,128)S(1)}, s32[2,4,1,1]{1,3,2,0:T(1,128)}, u32[]{:S(2)}) copy-start(s32[2,4,1,1]{1,3,2,0:T(1,128)} %param.6) | copy-start | bytes 100
  12.5 28.1 %collective-permute-start.1 = (f32[4,130,1024]{2,0,1:T(4,128)}, f32[4,130,1024]{2,0,1:T(4,128)}, u32[]{:S(2)}, u32[]{:S(2)}) collective-permute-start(f32[4,130,1024]{2,0,1:T(4,128)} %copy.43), channel_id=1, source_target_pairs={{8,0},{16,8},{24,16},{32,24},{40,32},{48,40},{56,48},{64,56},{72,6... | collective-permute-start | bytes 6389768 | tf_op jit(solution)/shard_map/ppermute | solution.py:26
  46.8 9.3 %copy-start.4 = (s32[2,4,1,1]{1,3,2,0:T(1,128)S(1)}, s32[2,4,1,1]{1,3,2,0:T(1,128)}, u32[]{:S(2)}) copy-start(s32[2,4,1,1]{1,3,2,0:T(1,128)} %param.7) | copy-start | bytes 100
  46.8 50.1 %copy-start.2 = (f32[4,256,1024]{1,0,2:T(4,128)S(1)}, f32[4,256,1024]{1,0,2:T(4,128)}, u32[]{:S(2)}) copy-start(f32[4,256,1024]{1,0,2:T(4,128)} %copy.28) | copy-start | bytes 12582916
  50.3 46.6 %collective-permute-start.2 = (f32[4,516,130]{1,0,2:T(4,128)S(1)}, f32[4,516,130]{1,0,2:T(4,128)S(1)}, u32[]{:S(2)}, u32[]{:S(2)}) collective-permute-start(f32[4,516,130]{1,0,2:T(4,128)S(1)} %get-tuple-element.42), channel_id=1, source_target_pairs={{0,1},{1,2},{2,3},{3,4},{4,5},{5,6},{6,7},{8,9},{9,10},{10,11},{11... | collective-permute-start | bytes 3219848 | tf_op jit(solution)/shard_map/ppermute | solution.py:25
  54.1 42.8 %collective-permute-start.3 = (f32[4,516,130]{1,0,2:T(4,128)S(1)}, f32[4,516,130]{1,0,2:T(4,128)S(1)}, u32[]{:S(2)}, u32[]{:S(2)}) collective-permute-start(f32[4,516,130]{1,0,2:T(4,128)S(1)} %get-tuple-element.43), channel_id=1, source_target_pairs={{1,0},{2,1},{3,2},{4,3},{5,4},{6,5},{7,6},{9,8},{10,9},{11,10},{12... | collective-permute-start | bytes 3219848 | tf_op jit(solution)/shard_map/ppermute | solution.py:26
  163.2 9.2 %copy-start.3 = (f32[4,256,1024]{2,1,0:T(8,128)S(1)}, f32[4,256,1024]{2,1,0:T(8,128)}, u32[]{:S(2)}) copy-start(f32[4,256,1024]{2,1,0:T(8,128)} %param.4) | copy-start | bytes 12582916
  175.9 24.1 %copy-start = (f32[4,256,1024]{2,1,0:T(8,128)}, f32[4,256,1024]{2,1,0:T(8,128)S(1)}, u32[]{:S(2)}) copy-start(f32[4,256,1024]{2,1,0:T(8,128)S(1)} %fusion.25) | copy-start | bytes 12582916
  176.0 19.8 %collective-permute-start.4 = (f32[4,4,1024]{2,1,0:T(4,128)S(1)}, f32[4,4,1024]{2,1,0:T(4,128)S(1)}, u32[]{:S(2)}, u32[]{:S(2)}) collective-permute-start(f32[4,4,1024]{2,1,0:T(4,128)S(1)} %get-tuple-element.53), channel_id=1, source_target_pairs={{0,8},{8,16},{16,24},{24,32},{32,40},{40,48},{48,56},{56,64},{64,7... | collective-permute-start | bytes 196616 | tf_op jit(solution)/shard_map/ppermute | solution.py:25
  193.8 5.6 %collective-permute-start.5 = (f32[4,4,1024]{2,1,0:T(4,128)S(1)}, f32[4,4,1024]{2,1,0:T(4,128)S(1)}, u32[]{:S(2)}, u32[]{:S(2)}) collective-permute-start(f32[4,4,1024]{2,1,0:T(4,128)S(1)} %get-tuple-element.54), channel_id=1, source_target_pairs={{8,0},{16,8},{24,16},{32,24},{40,32},{48,40},{56,48},{64,56},{72,6... | collective-permute-start | bytes 196616 | tf_op jit(solution)/shard_map/ppermute | solution.py:26
  200.4 5.9 %collective-permute-start.6 = (f32[4,264,4]{1,2,0:T(4,128)S(1)}, f32[4,264,4]{1,2,0:T(4,128)S(1)}, u32[]{:S(2)}, u32[]{:S(2)}) collective-permute-start(f32[4,264,4]{1,2,0:T(4,128)S(1)} %copy.32), channel_id=1, source_target_pairs={{0,1},{1,2},{2,3},{3,4},{4,5},{5,6},{6,7},{8,9},{9,10},{10,11},{11... | collective-permute-start | bytes 50696 | tf_op jit(solution)/shard_map/ppermute | solution.py:25
  204.8 4.8 %collective-permute-start.7 = (f32[4,264,4]{1,2,0:T(4,128)S(1)}, f32[4,264,4]{1,2,0:T(4,128)S(1)}, u32[]{:S(2)}, u32[]{:S(2)}) collective-permute-start(f32[4,264,4]{1,2,0:T(4,128)S(1)} %copy.34), channel_id=1, source_target_pairs={{1,0},{2,1},{3,2},{4,3},{5,4},{6,5},{7,6},{9,8},{10,9},{11,10},{12... | collective-permute-start | bytes 50696 | tf_op jit(solution)/shard_map/ppermute | solution.py:26
  327.3 4.4 collective-permute-start.8
  329.3 4.9 %collective-permute-start.9 = (f32[4,1,64]{2,1,0:T(1,128)S(1)}, f32[4,1,64]{2,1,0:T(1,128)S(1)}, u32[]{:S(2)}, u32[]{:S(2)}) collective-permute-start(f32[4,1,64]{2,1,0:T(1,128)S(1)} %get-tuple-element.60), channel_id=1, source_target_pairs={{8,0},{16,8},{24,16},{32,24},{40,32},{48,40},{56,48},{64,56},{72,6... | collective-permute-start | bytes 3080 | tf_op jit(solution)/shard_map/ppermute | solution.py:26
  334.3 3.4 collective-permute-start.10
  336.1 4.8 %collective-permute-start.11 = (f32[4,18,1]{2,1,0:T(8,128)S(1)}, f32[4,18,1]{2,1,0:T(8,128)S(1)}, u32[]{:S(2)}, u32[]{:S(2)}) collective-permute-start(f32[4,18,1]{2,1,0:T(8,128)S(1)} %get-tuple-element.58), channel_id=1, source_target_pairs={{1,0},{2,1},{3,2},{4,3},{5,4},{6,5},{7,6},{9,8},{10,9},{11,10},{12... | collective-permute-start | bytes 872 | tf_op jit(solution)/shard_map/ppermute | solution.py:26
  347.5 8.5 %copy-start.1 = (f32[4,256,1024]{2,1,0:T(8,128)}, f32[4,256,1024]{2,1,0:T(8,128)S(1)}, u32[]{:S(2)}) copy-start(f32[4,256,1024]{2,1,0:T(8,128)S(1)} %convolution_subtract_fusion) | copy-start | bytes 12582916
  347.5 5.3 %collective-permute-start.12 = (f32[4,1,1024]{2,1,0:T(1,128)S(1)}, f32[4,1,1024]{2,1,0:T(1,128)S(1)}, u32[]{:S(2)}, u32[]{:S(2)}) collective-permute-start(f32[4,1,1024]{2,1,0:T(1,128)S(1)} %get-tuple-element.52), channel_id=1, source_target_pairs={{0,8},{8,16},{16,24},{24,32},{32,40},{40,48},{48,56},{56,64},{64,7... | collective-permute-start | bytes 49160 | tf_op jit(solution)/shard_map/ppermute | solution.py:25
  350.9 5.1 %collective-permute-start.13 = (f32[4,1,1024]{2,1,0:T(1,128)S(1)}, f32[4,1,1024]{2,1,0:T(1,128)S(1)}, u32[]{:S(2)}, u32[]{:S(2)}) collective-permute-start(f32[4,1,1024]{2,1,0:T(1,128)S(1)} %get-tuple-element.51), channel_id=1, source_target_pairs={{8,0},{16,8},{24,16},{32,24},{40,32},{48,40},{56,48},{64,56},{72,6... | collective-permute-start | bytes 49160 | tf_op jit(solution)/shard_map/ppermute | solution.py:26
  356.5 5.6 %collective-permute-start.14 = (f32[4,258,1]{1,0,2:T(4,128)S(1)}, f32[4,258,1]{1,0,2:T(4,128)S(1)}, u32[]{:S(2)}, u32[]{:S(2)}) collective-permute-start(f32[4,258,1]{1,0,2:T(4,128)S(1)} %copy.38), channel_id=1, source_target_pairs={{1,0},{2,1},{3,2},{4,3},{5,4},{6,5},{7,6},{9,8},{10,9},{11,10},{12... | collective-permute-start | bytes 12392 | tf_op jit(solution)/shard_map/ppermute | solution.py:26
  358.1 4.8 %collective-permute-start.15 = (f32[4,258,1]{1,0,2:T(4,128)S(1)}, f32[4,258,1]{1,0,2:T(4,128)S(1)}, u32[]{:S(2)}, u32[]{:S(2)}) collective-permute-start(f32[4,258,1]{1,0,2:T(4,128)S(1)} %copy.40), channel_id=1, source_target_pairs={{0,1},{1,2},{2,3},{3,4},{4,5},{5,6},{6,7},{8,9},{9,10},{10,11},{11... | collective-permute-start | bytes 12392 | tf_op jit(solution)/shard_map/ppermute | solution.py:25
where the time goes:
time: 458 us; the launch traced here: 456 us
  blocking collectives  134 us (29%)
  other arithmetic  102 us (22%)
  local copies, waits for them, and re-layouts  83.4 us (18%)
  waiting for transfers between devices  71.2 us (16%)
  starting transfers between devices  55.5 us (12%)
  matrix products  8.74 us (2%)
    psum x1, blocking collectives, body(): height_all, slope_all = lax.psum((height_sq, slope_sum), ('row', 'col'))  78.1 us
    ppermute x8, waiting for transfers between devices, with_halo(): before = lax.ppermute(last, axis, up)  54.4 us
    ppermute x8, starting transfers between devices, with_halo(): before = lax.ppermute(last, axis, up)  41.4 us
    concatenate x4, other arithmetic, with_halo(): value = jnp.concatenate([before, value, after], axis=dim)  37.5 us
    all_gather x1, blocking collectives, long_cols(): portion = lax.all_gather(coarse, 'col', axis=2, tiled=True)  27.9 us
    all_gather x1, blocking collectives, long_rows(): portion = lax.all_gather(surface, 'row', axis=1, tiled=True)  27.6 us
    unnamed x18, local copies, waits for them, and re-layouts  24.7 us
    gather x12, local copies, waits for them, and re-layouts  21.5 us
  transfers between devices with their start and end apart: 16, of which 9 were waited for; matrix products, arithmetic and copies ran while one was open for 4% of the time, Pallas kernels for 0%

commit v1 on v0

--- a/solution.py
+++ b/solution.py
@@ -201,7 +201,9 @@
     slope_field = slopes(band_field)
     height_sq = jnp.sum(band_field * band_field, axis=(1, 2))
     slope_sum = jnp.sum(slope_field, axis=(1, 2))
-    height_all, slope_all = lax.psum((height_sq, slope_sum), ("row", "col"))
+    height_all, slope_all = lax.psum(
+        lax.psum((height_sq, slope_sum), axis_name="row"), axis_name="col"
+    )
     total_cells = height * lax.axis_size("row") * length * lax.axis_size("col")
     surface_params = jnp.sqrt(jnp.stack([height_all, slope_all]) / total_cells + EPSILON)
     return (band_field, slope_field, surface_params)

time: 458 us -> 445 us (0.972)
  the two profiles are of different devices: /device:TPU:1 before, /device:TPU:64 now
where the time goes in v1:
time: 445 us; the launch traced here: 443 us
  blocking collectives  111 us (25%)
  other arithmetic  102 us (23%)
  local copies, waits for them, and re-layouts  83.1 us (19%)
  waiting for transfers between devices  79.9 us (18%)
  starting transfers between devices  56.6 us (13%)
  matrix products  8.74 us (2%)
    ppermute x8, waiting for transfers between devices, with_halo(): before = lax.ppermute(last, axis, up)  66.9 us
    concatenate x4, other arithmetic, with_halo(): value = jnp.concatenate([before, value, after], axis=dim)  37.5 us
    psum x1, blocking collectives, body(): lax.psum((height_sq, slope_sum), axis_name='row')  37.2 us
    ppermute x8, starting transfers between devices, with_halo(): after = lax.ppermute(leading, axis, down)  34.6 us
    all_gather x1, blocking collectives, long_cols(): portion = lax.all_gather(coarse, 'col', axis=2, tiled=True)  32.9 us
    unnamed x18, local copies, waits for them, and re-layouts  24.7 us
    ppermute x8, starting transfers between devices, with_halo(): before = lax.ppermute(last, axis, up)  21.9 us
    gather x12, local copies, waits for them, and re-layouts  21.3 us
  transfers between devices with their start and end apart: 16, of which 9 were waited for; matrix products, arithmetic and copies ran while one was open for 4% of the time, Pallas kernels for 0%

profile of v1, /device:TPU:64, one launch (start us, length us, event | category | flops | bytes accessed | tf_op | source)
XLA Modules:
  0.0 442.8 jit_solution(17249186090269748911)
XLA Ops:
  0.6 3.2 fusion.118
  3.9 1.4 copy.42
  5.3 1.9 collective-permute-start
  7.2 2.7 copy.43
  9.9 7.4 %collective-permute-start.1 = (f32[4,130,1024]{2,0,1:T(4,128)}, f32[4,130,1024]{2,0,1:T(4,128)}, u32[]{:S(2)}, u32[]{:S(2)}) collective-permute-start(f32[4,130,1024]{2,0,1:T(4,128)} %copy.43), channel_id=1, source_target_pairs={{8,0},{16,8},{24,16},{32,24},{40,32},{48,40},{56,48},{64,56},{72,6... | collective-permute-start | bytes 6389768 | tf_op jit(solution)/shard_map/ppermute | solution.py:26
  17.3 5.2 %copy.28 = f32[4,256,1024]{1,0,2:T(4,128)} copy(f32[4,256,1024]{2,1,0:T(8,128)} %param.5) | data formatting | bytes 8388608 | tf_op args[1]
  22.7 14.0 %collective-permute-done = f32[4,130,1024]{2,0,1:T(4,128)} collective-permute-done((f32[4,130,1024]{2,0,1:T(4,128)S(1)}, f32[4,130,1024]{2,0,1:T(4,128)}, u32[]{:S(2)}, u32[]{:S(2)}) %collective-permute-start) | collective-permute-done | bytes 2129952 | tf_op jit(solution)/shard_map/ppermute | solution.py:25
  36.7 6.3 %copy.27 = f32[4,130,1024]{1,0,2:T(4,128)} copy(f32[4,130,1024]{2,0,1:T(4,128)} %collective-permute-done) | data formatting | bytes 4259840 | tf_op jit(solution)/shard_map/ppermute | solution.py:25
  42.9 6.2 %copy.29 = f32[4,130,1024]{1,0,2:T(4,128)} copy(f32[4,130,1024]{2,0,1:T(4,128)} %collective-permute-done.1) | data formatting | bytes 4259840 | tf_op jit(solution)/shard_map/ppermute | solution.py:26
  49.1 3.5 pad_maximum_fusion.13
  52.6 3.6 collective-permute-start.2
  56.2 1.5 collective-permute-start.3
  58.3 51.6 %collective-permute-done.2 = f32[4,516,130]{1,0,2:T(4,128)S(1)} collective-permute-done((f32[4,516,130]{1,0,2:T(4,128)S(1)}, f32[4,516,130]{1,0,2:T(4,128)S(1)}, u32[]{:S(2)}, u32[]{:S(2)}) %collective-permute-start.2) | collective-permute-done | bytes 1073312 | tf_op jit(solution)/shard_map/ppermute | solution.py:25
  110.0 29.5 %pad_maximum_fusion = f32[4,516,1284]{1,0,2:T(4,128)} fusion(f32[4,516,130]{1,0,2:T(4,128)S(1)} %collective-permute-done.3, f32[4,130,1024]{1,0,2:T(4,128)} %copy.29, f32[4,256,1024]{1,0,2:T(4,128)S(1)} %copy-done.2, f32[4,130,1024]{1,0,2:T(4,128)} %copy.27, f32[4,516,130]{1,0,2:T(4,128)S(1)} %collective-permute-done.2), kind=kLoop, calls=%fused_computation.2 | loop fusion | flops 10600704 | bytes 21201408 | tf_op jit(solution)/shard_map/concatenate | solution.py:27
  139.5 15.3 %copy.30 = f32[4,516,1284]{2,1,0:T(8,128)} copy(f32[4,516,1284]{1,0,2:T(4,128)} %pad_maximum_fusion) | data formatting | bytes 21201408
  154.7 21.3 %while.1 = (s32[]{:T(128)}, f32[4,516,1284]{2,1,0:T(8,128)}, s32[4,3]{1,0:T(4,128)S(1)}, f32[4,259,1027]{2,1,0:T(8,128)}, s32[]{:T(128)}) while((s32[]{:T(128)}, f32[4,516,1284]{2,1,0:T(8,128)}, s32[4,3]{1,0:T(4,128)S(1)}, f32[4,259,1027]{2,1,0:T(8,128)}, s32[]{:T(128)}) %tuple.51), condition=%wide.while_cond, body=%wide.while_body.sunk | while | flops 2 | bytes 2435185 | solution.py:68
  154.7 0.6 fusion.124
  155.3 4.8 %dynamic-slice_dynamic-update-slice_fusion.2 = f32[4,259,1027]{2,1,0:T(8,128)} fusion(f32[4,259,1027]{2,1,0:T(8,128)} %get-tuple-element.120, s32[]{:T(128)} %get-tuple-element.117, f32[4,516,1284]{2,1,0:T(8,128)} %get-tuple-element.123, s32[]{:T(128)} %bitcast.84, s32[]{:T(128)} %bitcast.85, s32[]{:T(128)} %bitcast.86), kind=kLoop, calls=%fused_computation.clone.1 | loop fusion | bytes 2435072 | tf_op jit(solution)/shard_map/vmap()/gather
  160.1 0.6 fusion.124
  160.7 4.7 %dynamic-slice_dynamic-update-slice_fusion.2 = f32[4,259,1027]{2,1,0:T(8,128)} fusion(f32[4,259,1027]{2,1,0:T(8,128)} %get-tuple-element.120, s32[]{:T(128)} %get-tuple-element.117, f32[4,516,1284]{2,1,0:T(8,128)} %get-tuple-element.123, s32[]{:T(128)} %bitcast.84, s32[]{:T(128)} %bitcast.85, s32[]{:T(128)} %bitcast.86), kind=kLoop, calls=%fused_computation.clone.1 | loop fusion | bytes 2435072 | tf_op jit(solution)/shard_map/vmap()/gather
  165.4 0.6 fusion.124
  166.0 4.7 %dynamic-slice_dynamic-update-slice_fusion.2 = f32[4,259,1027]{2,1,0:T(8,128)} fusion(f32[4,259,1027]{2,1,0:T(8,128)} %get-tuple-element.120, s32[]{:T(128)} %get-tuple-element.117, f32[4,516,1284]{2,1,0:T(8,128)} %get-tuple-element.123, s32[]{:T(128)} %bitcast.84, s32[]{:T(128)} %bitcast.85, s32[]{:T(128)} %bitcast.86), kind=kLoop, calls=%fused_computation.clone.1 | loop fusion | bytes 2435072 | tf_op jit(solution)/shard_map/vmap()/gather
  170.7 0.6 fusion.124
  171.3 4.7 %dynamic-slice_dynamic-update-slice_fusion.2 = f32[4,259,1027]{2,1,0:T(8,128)} fusion(f32[4,259,1027]{2,1,0:T(8,128)} %get-tuple-element.120, s32[]{:T(128)} %get-tuple-element.117, f32[4,516,1284]{2,1,0:T(8,128)} %get-tuple-element.123, s32[]{:T(128)} %bitcast.84, s32[]{:T(128)} %bitcast.85, s32[]{:T(128)} %bitcast.86), kind=kLoop, calls=%fused_computation.clone.1 | loop fusion | bytes 2435072 | tf_op jit(solution)/shard_map/vmap()/gather
  176.1 9.2 %multiply_add_fusion = f32[4,256,1027]{2,1,0:T(8,128)S(1)} fusion(f32[4,259,1027]{2,1,0:T(8,128)} %get-tuple-element.10, f32[4]{0:T(128)S(1)} %get-tuple-element.69, f32[4]{0:T(128)S(1)} %get-tuple-element.64, f32[4]{0:T(128)S(1)} %get-tuple-element.66, f32[4]{0:T(128)S(1)} %get-tuple-element.65), kind=kLoop, calls=%fused_computation.5 | loop fusion | flops 7361536 | bytes 21033024 | tf_op jit(solution)/shard_map/vmap()/add | solution.py:47
  185.3 3.4 fusion.25
  188.8 1.9 collective-permute-start.4
  190.7 7.3 %collective-permute-start.5 = (f32[4,4,1024]{2,1,0:T(4,128)S(1)}, f32[4,4,1024]{2,1,0:T(4,128)S(1)}, u32[]{:S(2)}, u32[]{:S(2)}) collective-permute-start(f32[4,4,1024]{2,1,0:T(4,128)S(1)} %get-tuple-element.56), channel_id=1, source_target_pairs={{8,0},{16,8},{24,16},{32,24},{40,32},{48,40},{56,48},{64,56},{72,6... | collective-permute-start | bytes 196616 | tf_op jit(solution)/shard_map/ppermute | solution.py:26
  198.0 1.9 collective-permute-done.5
  199.9 0.6 pad_maximum_fusion.2
  200.6 0.3 copy.32
  200.9 4.4 collective-permute-start.6
  205.3 0.3 copy.34
  205.6 1.5 collective-permute-start.7
  207.4 4.2 collective-permute-done.7
  211.8 7.4 %maximum_maximum_fusion = (f32[4,264,1028]{2,1,0:T(8,128)S(1)}, f32[4,264,1028]{2,1,0:T(8,128)}) fusion(f32[4,4,1024]{2,1,0:T(4,128)S(1)} %collective-permute-done.5, f32[4,256,1024]{2,1,0:T(8,128)} %copy-done, f32[4,4,1024]{2,1,0:T(4,128)S(1)} %collective-permute-done.4, f32[4,264,4]{2,1,0:T(8,128)S(1)} %copy.33, f32[4,264,4]{2,1,0:T(8,128)S(1)} %copy.35), kind=kLoop, calls=%fused_computation.3 | loop fusion | flops 6513408 | bytes 13043712 | tf_op jit(solution)/shard_map/concatenate | solution.py:27
  219.3 15.3 %fusion.1 = f32[4,264,1024]{2,1,0:T(8,128)S(1)} fusion(f32[4,264,1028]{2,1,0:T(8,128)} %get-tuple-element.47, f32[4,264,1028]{2,1,0:T(8,128)S(1)} %get-tuple-element.46, f32[1024]{0:T(1024)S(1)} %fusion.80, f32[4,4,1024]{2,1,0:T(4,128)S(1)} %collective-permute-done.5, f32[4,256,1024]{2,1,0:T(8,128)} %copy-done, f32[4,4,1024]{2,1,0:T(4,128)S(1)} %collective-permute-done.4), kind=kLoop, calls=%fused_computation.8 | loop fusion | flops 20545536 | bytes 43257856 | tf_op jit(solution)/shard_map/div | solution.py:95
  234.6 5.7 %fusion.17 = f32[4,256,1024]{2,1,0:T(8,128)} fusion(f32[4,264,1024]{2,1,0:T(8,128)S(1)} %fusion.1, f32[256]{0:T(256)S(1)} %multiply_add_fusion.3), kind=kLoop, calls=%fused_computation.41 | loop fusion | flops 17825792 | bytes 41944064 | tf_op jit(solution)/shard_map/div | solution.py:105
  240.2 19.0 %reshape.249 = f32[4,16,16,64,16]{4,3,2,1,0:T(8,128)} reshape(f32[4,256,1024]{2,1,0:T(8,128)} %fusion.17) | data formatting | bytes 8388608 | tf_op jit(solution)/shard_map/reshape | solution.py:110
  259.2 12.2 %reduce_sum.45 = f32[4,16,64]{2,1,0:T(8,128)S(1)} reduce(f32[4,16,16,64,16]{4,3,2,1,0:T(8,128)} %reshape.249, f32[]{:T(128)} %constant.64.clone.1), dimensions={2,4}, to_apply=%region_0.0 | reduce | flops 1044480 | bytes 4210692 | tf_op jit(solution)/shard_map/reduce_sum | solution.py:110
  271.5 32.9 %all_gather.6 = f32[4,16,512]{1,0,2:T(4,128)S(1)} all-gather(f32[4,16,64]{1,0,2:T(4,128)S(1)} %copy.36), channel_id=1, replica_groups=mesh['row'=16,'col'=8] {'col'}, dimensions={2}, use_global_device_ids=true | all-gather | bytes 147456 | tf_op jit(solution)/shard_map/all_gather | solution.py:121
  304.5 1.8 convolution_divide_fusion
  306.2 20.5 %all_gather.7 = f32[4,256,64]{2,1,0:T(8,128)S(1)} all-gather(f32[4,16,64]{2,1,0:T(8,128)S(1)} %convolution_divide_fusion), channel_id=1, replica_groups=mesh['row'=16,'col'=8] {'row'}, dimensions={1}, use_global_device_ids=true | all-gather | bytes 278528 | tf_op jit(solution)/shard_map/all_gather | solution.py:132
  326.8 0.4 fusion.28
  327.2 2.3 collective-permute-start.8
  329.5 6.9 %collective-permute-start.9 = (f32[4,1,64]{2,1,0:T(1,128)S(1)}, f32[4,1,64]{2,1,0:T(1,128)S(1)}, u32[]{:S(2)}, u32[]{:S(2)}) collective-permute-start(f32[4,1,64]{2,1,0:T(1,128)S(1)} %get-tuple-element.62), channel_id=1, source_target_pairs={{8,0},{16,8},{24,16},{32,24},{40,32},{48,40},{56,48},{64,56},{72,6... | collective-permute-start | bytes 3080 | tf_op jit(solution)/shard_map/ppermute | solution.py:26
  336.4 1.3 collective-permute-done.9
  337.8 1.3 collective-permute-start.10
  339.1 1.6 collective-permute-start.11
  340.8 4.3 collective-permute-done.11
  345.0 0.6 convolution_bitcast_fusion
  345.6 6.0 %convolution_subtract_fusion = f32[4,256,1024]{2,1,0:T(8,128)S(1)} fusion(f32[4,256,1024]{2,1,0:T(8,128)} %fusion.17, f32[4,256,66]{1,2,0:T(8,128)S(1)} %convolution_bitcast_fusion, f32[1024]{0:T(1024)S(1)} %get-tuple-element.73, s32[1024]{0:T(1024)S(1)} %get-tuple-element.76, f32[1024]{0:T(1024)S(1)} %get-tuple-element.74, ...), kind=kOutput, calls=%fused_computation.65 | convolution fusion | flops 831858688 | bytes 8675592 | tf_op jit(solution)/shard_map/spb,qb->spq/dot_general | solution.py:170
  351.6 1.9 collective-permute-start.12
  353.6 7.3 %collective-permute-start.13 = (f32[4,1,1024]{2,1,0:T(1,128)S(1)}, f32[4,1,1024]{2,1,0:T(1,128)S(1)}, u32[]{:S(2)}, u32[]{:S(2)}) collective-permute-start(f32[4,1,1024]{2,1,0:T(1,128)S(1)} %get-tuple-element.53), channel_id=1, source_target_pairs={{8,0},{16,8},{24,16},{32,24},{40,32},{48,40},{56,48},{64,56},{72,6... | collective-permute-start | bytes 49160 | tf_op jit(solution)/shard_map/ppermute | solution.py:26
  360.9 1.4 collective-permute-done.13
  362.5 0.3 copy.38
  362.8 1.3 collective-permute-start.14
  364.1 0.3 copy.40
  364.3 4.6 %collective-permute-start.15 = (f32[4,258,1]{1,0,2:T(4,128)S(1)}, f32[4,258,1]{1,0,2:T(4,128)S(1)}, u32[]{:S(2)}, u32[]{:S(2)}) collective-permute-start(f32[4,258,1]{1,0,2:T(4,128)S(1)} %copy.40), channel_id=1, source_target_pairs={{0,1},{1,2},{2,3},{3,4},{4,5},{5,6},{6,7},{8,9},{9,10},{10,11},{11... | collective-permute-start | bytes 12392 | tf_op jit(solution)/shard_map/ppermute | solution.py:25
  369.2 1.1 collective-permute-done.15
  370.5 13.9 %fusion.112 = (f32[4]{0:T(128)S(1)}, f32[4,256,1024]{2,1,0:T(8,128)}, f32[4]{0:T(128)S(1)}) fusion(f32[256]{0:T(256)S(1)} %and_convert_fusion, f32[4,256,1024]{2,1,0:T(8,128)} %copy-done.1, f32[4,1,1024]{2,1,0:T(1,128)S(1)} %collective-permute-done.12, f32[4,1,1024]{2,1,0:T(1,128)S(1)} %collective-permute-done.13, f32[1024]{0:T(1024)S(1)} %fusion.92, ...), kind=kLoop, calls=%fused_computation.219 | loop fusion | flops 18874360 | bytes 8434784 | tf_op jit(solution)/shard_map/reduce_sum | solution.py:203
  384.4 37.2 %all-reduce = (f32[4]{0:T(128)S(1)}, f32[4]{0:T(128)S(1)}) all-reduce(f32[4]{0:T(128)S(1)} %get-tuple-element.39, f32[4]{0:T(128)S(1)} %get-tuple-element.52), channel_id=1, replica_groups=mesh['row'=16,'col'=8] {'row'}, use_global_device_ids=true, to_apply=%region_7.8 | all-reduce | flops 8 | bytes 64 | tf_op jit(solution)/shard_map/psum | solution.py:205
  421.7 20.6 %all-reduce.1 = (f32[1,4]{1,0:T(1,128)S(1)}, f32[1,4]{1,0:T(1,128)S(1)}) all-reduce(f32[1,4]{1,0:T(1,128)S(1)} %bitcast.87, f32[1,4]{1,0:T(1,128)S(1)} %bitcast.88), channel_id=1, replica_groups=mesh['row'=16,'col'=8] {'col'}, use_global_device_ids=true, to_apply=%region_8.9 | all-reduce | flops 8 | bytes 64 | tf_op jit(solution)/shard_map/psum | solution.py:204
  442.3 0.6 fusion.98
  (59 shorter events, 2.7 us)
Async XLA Ops:
  5.3 31.4 %collective-permute-start = (f32[4,130,1024]{2,0,1:T(4,128)S(1)}, f32[4,130,1024]{2,0,1:T(4,128)}, u32[]{:S(2)}, u32[]{:S(2)}) collective-permute-start(f32[4,130,1024]{2,0,1:T(4,128)S(1)} %copy.42), channel_id=1, source_target_pairs={{0,8},{8,16},{16,24},{24,32},{32,40},{40,48},{48,56},{56,64},{64,7... | collective-permute-start | bytes 6389768 | tf_op jit(solution)/shard_map/ppermute | solution.py:25
  9.9 12.6 %copy-start.5 = (s32[2,4,1,1]{1,3,2,0:T(1,128)S(1)}, s32[2,4,1,1]{1,3,2,0:T(1,128)}, u32[]{:S(2)}) copy-start(s32[2,4,1,1]{1,3,2,0:T(1,128)} %param.6) | copy-start | bytes 100
  9.9 33.0 %collective-permute-start.1 = (f32[4,130,1024]{2,0,1:T(4,128)}, f32[4,130,1024]{2,0,1:T(4,128)}, u32[]{:S(2)}, u32[]{:S(2)}) collective-permute-start(f32[4,130,1024]{2,0,1:T(4,128)} %copy.43), channel_id=1, source_target_pairs={{8,0},{16,8},{24,16},{32,24},{40,32},{48,40},{56,48},{64,56},{72,6... | collective-permute-start | bytes 6389768 | tf_op jit(solution)/shard_map/ppermute | solution.py:26
  49.1 9.1 %copy-start.4 = (s32[2,4,1,1]{1,3,2,0:T(1,128)S(1)}, s32[2,4,1,1]{1,3,2,0:T(1,128)}, u32[]{:S(2)}) copy-start(s32[2,4,1,1]{1,3,2,0:T(1,128)} %param.7) | copy-start | bytes 100
  49.1 60.9 %copy-start.2 = (f32[4,256,1024]{1,0,2:T(4,128)S(1)}, f32[4,256,1024]{1,0,2:T(4,128)}, u32[]{:S(2)}) copy-start(f32[4,256,1024]{1,0,2:T(4,128)} %copy.28) | copy-start | bytes 12582916
  52.6 57.4 %collective-permute-start.2 = (f32[4,516,130]{1,0,2:T(4,128)S(1)}, f32[4,516,130]{1,0,2:T(4,128)S(1)}, u32[]{:S(2)}, u32[]{:S(2)}) collective-permute-start(f32[4,516,130]{1,0,2:T(4,128)S(1)} %get-tuple-element.44), channel_id=1, source_target_pairs={{0,1},{1,2},{2,3},{3,4},{4,5},{5,6},{6,7},{8,9},{9,10},{10,11},{11... | collective-permute-start | bytes 3219848 | tf_op jit(solution)/shard_map/ppermute | solution.py:25
  56.2 53.8 %collective-permute-start.3 = (f32[4,516,130]{1,0,2:T(4,128)S(1)}, f32[4,516,130]{1,0,2:T(4,128)S(1)}, u32[]{:S(2)}, u32[]{:S(2)}) collective-permute-start(f32[4,516,130]{1,0,2:T(4,128)S(1)} %get-tuple-element.45), channel_id=1, source_target_pairs={{1,0},{2,1},{3,2},{4,3},{5,4},{6,5},{7,6},{9,8},{10,9},{11,10},{12... | collective-permute-start | bytes 3219848 | tf_op jit(solution)/shard_map/ppermute | solution.py:26
  176.1 9.2 %copy-start.3 = (f32[4,256,1024]{2,1,0:T(8,128)S(1)}, f32[4,256,1024]{2,1,0:T(8,128)}, u32[]{:S(2)}) copy-start(f32[4,256,1024]{2,1,0:T(8,128)} %param.4) | copy-start | bytes 12582916
  188.7 11.7 %copy-start = (f32[4,256,1024]{2,1,0:T(8,128)}, f32[4,256,1024]{2,1,0:T(8,128)S(1)}, u32[]{:S(2)}) copy-start(f32[4,256,1024]{2,1,0:T(8,128)S(1)} %fusion.25) | copy-start | bytes 12582916
  188.8 9.2 %collective-permute-start.4 = (f32[4,4,1024]{2,1,0:T(4,128)S(1)}, f32[4,4,1024]{2,1,0:T(4,128)S(1)}, u32[]{:S(2)}, u32[]{:S(2)}) collective-permute-start(f32[4,4,1024]{2,1,0:T(4,128)S(1)} %get-tuple-element.55), channel_id=1, source_target_pairs={{0,8},{8,16},{16,24},{24,32},{32,40},{40,48},{48,56},{56,64},{64,7... | collective-permute-start | bytes 196616 | tf_op jit(solution)/shard_map/ppermute | solution.py:25
  190.7 9.1 %collective-permute-start.5 = (f32[4,4,1024]{2,1,0:T(4,128)S(1)}, f32[4,4,1024]{2,1,0:T(4,128)S(1)}, u32[]{:S(2)}, u32[]{:S(2)}) collective-permute-start(f32[4,4,1024]{2,1,0:T(4,128)S(1)} %get-tuple-element.56), channel_id=1, source_target_pairs={{8,0},{16,8},{24,16},{32,24},{40,32},{48,40},{56,48},{64,56},{72,6... | collective-permute-start | bytes 196616 | tf_op jit(solution)/shard_map/ppermute | solution.py:26
  200.9 6.2 %collective-permute-start.6 = (f32[4,264,4]{1,2,0:T(4,128)S(1)}, f32[4,264,4]{1,2,0:T(4,128)S(1)}, u32[]{:S(2)}, u32[]{:S(2)}) collective-permute-start(f32[4,264,4]{1,2,0:T(4,128)S(1)} %copy.32), channel_id=1, source_target_pairs={{0,1},{1,2},{2,3},{3,4},{4,5},{5,6},{6,7},{8,9},{9,10},{10,11},{11... | collective-permute-start | bytes 50696 | tf_op jit(solution)/shard_map/ppermute | solution.py:25
  205.6 6.0 %collective-permute-start.7 = (f32[4,264,4]{1,2,0:T(4,128)S(1)}, f32[4,264,4]{1,2,0:T(4,128)S(1)}, u32[]{:S(2)}, u32[]{:S(2)}) collective-permute-start(f32[4,264,4]{1,2,0:T(4,128)S(1)} %copy.34), channel_id=1, source_target_pairs={{1,0},{2,1},{3,2},{4,3},{5,4},{6,5},{7,6},{9,8},{10,9},{11,10},{12... | collective-permute-start | bytes 50696 | tf_op jit(solution)/shard_map/ppermute | solution.py:26
  327.2 9.2 %collective-permute-start.8 = (f32[4,1,64]{2,1,0:T(1,128)S(1)}, f32[4,1,64]{2,1,0:T(1,128)S(1)}, u32[]{:S(2)}, u32[]{:S(2)}) collective-permute-start(f32[4,1,64]{2,1,0:T(1,128)S(1)} %get-tuple-element.61), channel_id=1, source_target_pairs={{0,8},{8,16},{16,24},{24,32},{32,40},{40,48},{48,56},{56,64},{64,7... | collective-permute-start | bytes 3080 | tf_op jit(solution)/shard_map/ppermute | solution.py:25
  329.5 8.2 %collective-permute-start.9 = (f32[4,1,64]{2,1,0:T(1,128)S(1)}, f32[4,1,64]{2,1,0:T(1,128)S(1)}, u32[]{:S(2)}, u32[]{:S(2)}) collective-permute-start(f32[4,1,64]{2,1,0:T(1,128)S(1)} %get-tuple-element.62), channel_id=1, source_target_pairs={{8,0},{16,8},{24,16},{32,24},{40,32},{48,40},{56,48},{64,56},{72,6... | collective-permute-start | bytes 3080 | tf_op jit(solution)/shard_map/ppermute | solution.py:26
  337.8 3.0 collective-permute-start.10
  339.1 6.0 %collective-permute-start.11 = (f32[4,18,1]{2,1,0:T(8,128)S(1)}, f32[4,18,1]{2,1,0:T(8,128)S(1)}, u32[]{:S(2)}, u32[]{:S(2)}) collective-permute-start(f32[4,18,1]{2,1,0:T(8,128)S(1)} %get-tuple-element.60), channel_id=1, source_target_pairs={{1,0},{2,1},{3,2},{4,3},{5,4},{6,5},{7,6},{9,8},{10,9},{11,10},{12... | collective-permute-start | bytes 872 | tf_op jit(solution)/shard_map/ppermute | solution.py:26
  351.6 10.7 %copy-start.1 = (f32[4,256,1024]{2,1,0:T(8,128)}, f32[4,256,1024]{2,1,0:T(8,128)S(1)}, u32[]{:S(2)}) copy-start(f32[4,256,1024]{2,1,0:T(8,128)S(1)} %convolution_subtract_fusion) | copy-start | bytes 12582916
  351.6 9.2 %collective-permute-start.12 = (f32[4,1,1024]{2,1,0:T(1,128)S(1)}, f32[4,1,1024]{2,1,0:T(1,128)S(1)}, u32[]{:S(2)}, u32[]{:S(2)}) collective-permute-start(f32[4,1,1024]{2,1,0:T(1,128)S(1)} %get-tuple-element.54), channel_id=1, source_target_pairs={{0,8},{8,16},{16,24},{24,32},{32,40},{40,48},{48,56},{56,64},{64,7... | collective-permute-start | bytes 49160 | tf_op jit(solution)/shard_map/ppermute | solution.py:25
  353.6 8.7 %collective-permute-start.13 = (f32[4,1,1024]{2,1,0:T(1,128)S(1)}, f32[4,1,1024]{2,1,0:T(1,128)S(1)}, u32[]{:S(2)}, u32[]{:S(2)}) collective-permute-start(f32[4,1,1024]{2,1,0:T(1,128)S(1)} %get-tuple-element.53), channel_id=1, source_target_pairs={{8,0},{16,8},{24,16},{32,24},{40,32},{48,40},{56,48},{64,56},{72,6... | collective-permute-start | bytes 49160 | tf_op jit(solution)/shard_map/ppermute | solution.py:26
  362.8 6.2 %collective-permute-start.14 = (f32[4,258,1]{1,0,2:T(4,128)S(1)}, f32[4,258,1]{1,0,2:T(4,128)S(1)}, u32[]{:S(2)}, u32[]{:S(2)}) collective-permute-start(f32[4,258,1]{1,0,2:T(4,128)S(1)} %copy.38), channel_id=1, source_target_pairs={{1,0},{2,1},{3,2},{4,3},{5,4},{6,5},{7,6},{9,8},{10,9},{11,10},{12... | collective-permute-start | bytes 12392 | tf_op jit(solution)/shard_map/ppermute | solution.py:26
  364.3 6.0 %collective-permute-start.15 = (f32[4,258,1]{1,0,2:T(4,128)S(1)}, f32[4,258,1]{1,0,2:T(4,128)S(1)}, u32[]{:S(2)}, u32[]{:S(2)}) collective-permute-start(f32[4,258,1]{1,0,2:T(4,128)S(1)} %copy.40), channel_id=1, source_target_pairs={{0,1},{1,2},{2,3},{3,4},{4,5},{5,6},{6,7},{8,9},{9,10},{10,11},{11... | collective-permute-start | bytes 12392 | tf_op jit(solution)/shard_map/ppermute | solution.py:25
